TPU v7x, 32 devices: a whole 2x2x4 slice. The times are simulated.
32 devices in a mesh: tm: 4 (over y, x), vox: 8 (over z, core).
Axes of the slice: x: 2, y: 2, z: 4, core: 2. Of those that a mesh axis runs over, the one named last changes fastest.
Arguments:
- u_train: bfloat16 [3072, 4096], P('tm'), may hold values from -0.109375 to 0.109375
- y_train: bfloat16 [3072, 3072], P('tm', 'vox'), may hold values from -6 to 6
- sing: float32 [4096], replicated, may hold values from 0.5 to 8
- lambdas: float32 [20], replicated, may hold values from 0.1 to 100
- lam_index: int32 [24], P('vox'), may hold values from 0 to 19
- live: int32 [24], P('vox'), may hold values from 0 to 1, as said below
- v_basis: bfloat16 [4096, 4096], P('tm', 'vox'), may hold values from -0.09375 to 0.09375
- x_test: bfloat16 [1024, 4096], P(None, 'tm'), may hold values from -0.09375 to 0.09375
Outputs:
- weights: bfloat16 [4096, 3072], P('tm', 'vox')
- predictions: bfloat16 [1024, 3072], P('tm', 'vox')
Inputs may be any that keep to these rules, and one draw needn't show every extreme that they name: Of the 3 voxel blocks that one device along vox holds, at most 2 are live, and some device holds exactly 2.
All inputs are finite; a program needn't handle non-finite values.
Results may differ from a plain program's by a relative error of at most 0.0058.
Values may be sent and summed in bfloat16 or wider, within the bound.
A program may use at most 128 MiB of HBM per device.

v0:
```python
import jax
import jax.numpy as jnp
from jax import lax
from jax.sharding import PartitionSpec as P

BLK = 128


def body(u_train, y_train, sing, lambdas, lam_index, live, v_basis, x_test):
    time_rows = y_train.shape[0]
    column_count = y_train.shape[1]
    block_count = lam_index.shape[0]
    penalty_count = lambdas.shape[0]
    capacity = block_count - block_count // 3
    selector = (lam_index[:, None] == jnp.arange(penalty_count, dtype=jnp.int32)[None, :]).astype(
        jnp.float32
    )
    selector = selector * live[:, None].astype(jnp.float32)
    ranking = jnp.argsort((1 - live) * block_count + jnp.arange(block_count, dtype=jnp.int32))
    picked = ranking[:capacity]
    responses = jnp.take(y_train.reshape(time_rows, block_count, BLK), picked, axis=1)
    responses = responses.reshape(time_rows, capacity * BLK)
    used_selector = jnp.take(selector, picked, axis=0)
    used_columns = responses.shape[1]
    used_blocks = used_selector.shape[0]
    partial_value = lax.dot_general(
        u_train, responses, (((0,), (0,)), ((), ())), preferred_element_type=jnp.float32
    )
    products = lax.psum(partial_value, "tm")
    filters = sing[None, :] / (sing[None, :] * sing[None, :] + lambdas[:, None])
    row_count = products.shape[0]
    blocks = (
        products.reshape(row_count, used_blocks, BLK)
        * jnp.dot(used_selector, filters, precision=lax.Precision.HIGHEST).T[:, :, None]
    )
    filtered = blocks.reshape(row_count, used_columns).astype(jnp.bfloat16)
    weight_sum = jnp.dot(
        lax.all_gather(v_basis, "vox", axis=1, tiled=True),
        filtered,
        preferred_element_type=jnp.float32,
    )
    weight_cols = weight_sum.astype(jnp.bfloat16)
    partial_test = jnp.dot(x_test, weight_cols, preferred_element_type=jnp.float32)
    predicted = lax.psum_scatter(partial_test, "tm", scatter_dimension=0, tiled=True).astype(
        jnp.bfloat16
    )

    def expand(values):
        row_count = values.shape[0]
        placed = jnp.zeros((row_count, block_count, BLK), values.dtype)
        placed = placed.at[:, picked, :].set(values.reshape(row_count, capacity, BLK))
        return placed.reshape(row_count, column_count)

    return (expand(weight_cols), expand(predicted))


def solution(mesh):
    placed = (
        P("tm", None),
        P("tm", "vox"),
        P(),
        P(),
        P("vox"),
        P("vox"),
        P("tm", "vox"),
        P(None, "tm"),
    )
    return jax.shard_map(
        body,
        mesh=mesh,
        in_specs=placed,
        out_specs=(P("tm", "vox"), P("tm", "vox")),
        check_vma=False,
    )
```

profile of v0, /device:TPU:0, one launch (start us, length us, event | category | flops | bytes accessed | tf_op | source)
XLA Modules:
  0.0 177.4 jit_solution(16627243049810682810)
XLA Ops:
  8.0 0.0 all-reduce.2.cloned.1.call-start
  8.1 0.8 fusion.10
  8.9 0.7 sort.17
  9.6 1.3 copy.20
  10.9 0.3 copy.21
  11.3 1.3 gather_fusion
  12.6 1.2 copy.22
  13.8 0.1 broadcast_bitcast_fusion
  13.8 0.1 bitcast_select_fusion
  14.0 6.6 %convolution_bitcast_fusion = f32[4096,256]{0,1:T(8,128)} fusion(bf16[768,256]{0,1:T(8,128)(2,1)S(1)} %bitcast_select_fusion, bf16[768,4096]{1,0:T(8,128)(2,1)} %param.8), kind=kOutput, calls=%fused_computation.4 | convolution fusion | flops 1610612736 | bytes 10878976 | tf_op jit(solution)/shard_map/dot_general | solution.py:26
  20.6 0.0 all-reduce.2.cloned.1.call-update
  20.6 0.0 all-gather.2.cloned.1.call-start
  20.7 0.5 all-gather.2.cloned.1.call-update
  21.2 0.0 reduce-scatter.2.cloned.1.call-start
  21.3 0.1 fusion.5
  21.3 0.6 gather_fusion.1
  21.9 0.5 fusion.1
  22.4 104.7 %all-reduce.2.cloned.1.call-done = f32[4096,256]{0,1:T(8,128)} async-done(((f32[4096,256]{0,1:T(8,128)}), f32[4096,256]{0,1:T(8,128)}) %all-reduce.2.cloned.1.call-update) | async-done | bytes 4194320 | tf_op jit(solution)/shard_map/psum | solution.py:29
  127.1 3.9 %fusion = bf16[4096,256]{0,1:T(8,128)(2,1)} fusion(f32[4096,256]{0,1:T(8,128)} %all-reduce.2.cloned.1.call-done, f32[4096,2]{0,1:T(2,128)S(1)} %fusion.1), kind=kLoop, calls=%fused_computation.6 | loop fusion | flops 2097152 | bytes 6324224 | tf_op jit(solution)/shard_map/convert_element_type | solution.py:36
  131.0 6.4 %convolution_convert_fusion = bf16[256,1024]{1,0:T(8,128)(2,1)S(1)} fusion(bf16[4096,256]{0,1:T(8,128)(2,1)} %fusion, bf16[1024,4096]{1,0:T(8,128)(2,1)} %all-gather.2.cloned.1.call-done), kind=kOutput, calls=%fused_computation.8 | convolution fusion | flops 2147745792 | bytes 11010048 | tf_op jit(solution)/shard_map/dot_general | solution.py:37
  137.4 1.7 convolution_bitcast_fusion.1
  139.2 0.3 copy.23
  139.4 0.1 broadcast_in_dim.42
  139.6 0.7 scatter_fusion
  140.3 1.2 copy.24
  141.5 2.3 %copy.27 = bf16[1024,384]{1,0:T(8,128)(2,1)} copy(bf16[1024,384]{0,1:T(8,128)(2,1)} %bitcast.28) | data formatting | bytes 1572864
  143.8 23.4 %reduce-scatter.2.cloned.1.call-done = f32[256,256]{0,1:T(8,128)} async-done(((f32[1024,256]{0,1:T(8,128)}), f32[256,256]{0,1:T(8,128)}) %reduce-scatter.2.cloned.1.call-update) | async-done | bytes 262160 | tf_op jit(solution)/shard_map/reduce_scatter | solution.py:44
  167.3 1.0 convert_element_type.21
  168.2 0.1 copy.25
  168.4 0.6 scatter_fusion.1
  169.0 0.1 copy.26
  169.2 0.8 copy.28
  (15 shorter events, 0.1 us)
Async XLA Ops:
  8.0 129.4 %copy-start = (bf16[1024,1024]{1,0:T(8,128)(2,1)S(1)}, bf16[1024,1024]{1,0:T(8,128)(2,1)}, u32[]{:S(2)}) copy-start(bf16[1024,1024]{1,0:T(8,128)(2,1)} %param.15) | copy-start | bytes 6291460
  8.0 119.1 %all-reduce.2.cloned.1.call-start = ((), (), s32[]{:S(2)}) async-start(), calls=%async_computation.1 | async-start | bytes 8388608 | tf_op jit(solution)/shard_map/psum | solution.py:29
  20.6 0.7 copy-start.2
  20.6 1.3 copy-start.1
  20.6 1.3 copy-start.3
  20.6 110.4 %all-gather.2.cloned.1.call-start = ((), (), s32[]{:S(2)}) async-start(), calls=%async_computation.2 | async-start | bytes 9437184 | tf_op jit(solution)/shard_map/all_gather | solution.py:38
  21.2 146.1 %reduce-scatter.2.cloned.1.call-start = ((), (), s32[]{:S(2)}) async-start(), calls=%async_computation.3 | async-start | bytes 1310720 | tf_op jit(solution)/shard_map/reduce_scatter | solution.py:44
Sparse Core Ops, SparseCore 0:
  20.7 106.3 all-reduce.1
  139.3 27.9 reduce-scatter.1
Sparse Core Ops, SparseCore 1:
  22.7 84.6 all-gather.1
where the time goes:
time: 178 us; the launch traced here: 177 us
  waiting for transfers between devices  129 us (72%)
  between operations  15.6 us (9%)
  matrix products  15.2 us (9%)
  local copies, waits for them, and re-layouts  11.1 us (6%)
  other arithmetic  6.63 us (4%)
    psum x1, waiting for transfers between devices, body(): products = lax.psum(partial_value, 'tm')  105 us
    reduce_scatter x1, waiting for transfers between devices, body(): lax.psum_scatter(partial_test, 'tm', scatter_dimension=0, tiled=True)  23.4 us
    dot_general x1, matrix products, body(): lax.dot_general(u_train, responses, (((0,), (0,)), ((), ())), preferred_e...  6.63 us
    dot_general x1, matrix products, body(): jnp.dot(lax.all_gather(v_basis, 'vox', axis=1, tiled=True), filtered, pre...  6.38 us
    unnamed x11, local copies, waits for them, and re-layouts  4.43 us
    convert_element_type x1, other arithmetic, body(): filtered = blocks.reshape(row_count, used_columns).astype(jnp.bfloat16)  3.9 us
  transfers between devices with their start and end apart: 3, of which 2 were waited for; matrix products, arithmetic and copies ran while one was open for 5% of the time, Pallas kernels for 0%

commit v1 on v0

--- a/solution.py
+++ b/solution.py
@@ -26,7 +26,7 @@
     partial_value = lax.dot_general(
         u_train, responses, (((0,), (0,)), ((), ())), preferred_element_type=jnp.float32
     )
-    products = lax.psum(partial_value, "tm")
+    products = jnp.sum(lax.all_gather(partial_value, "tm"), axis=0)
     filters = sing[None, :] / (sing[None, :] * sing[None, :] + lambdas[:, None])
     row_count = products.shape[0]
     blocks = (

time: 178 us -> 309 us (1.74)
  waiting for transfers between devices: 129 us -> 225 us
  local copies, waits for them, and re-layouts: 11.1 us -> 31.9 us
  other arithmetic: 6.63 us -> 21.7 us
    all_gather x0 -> x1, waiting for transfers between devices: none -> 158 us  [body(): products = jnp.sum(lax.all_gather(partial_value, 'tm'), axis=0)]
    psum x1 -> x0, waiting for transfers between devices: 105 us -> none  [body(): products = lax.psum(partial_value, 'tm')]
    all_gather x1, waiting for transfers between devices: 0.01 us -> 44 us  [body(): lax.all_gather(v_basis, 'vox', axis=1, tiled=True)]
    all_gather x0 -> x1, local copies, waits for them, and re-layouts: none -> 20.7 us  [body(): products = jnp.sum(lax.all_gather(partial_value, 'tm'), axis=0)]
    reduce_sum x0 -> x1, other arithmetic: none -> 15.1 us  [body(): products = jnp.sum(lax.all_gather(partial_value, 'tm'), axis=0)]
  transfers between devices with their start and end apart: 3 -> 3, of which waited for: 2 -> 3; matrix products, arithmetic and copies ran while one was open for 5% -> 15% of each run, Pallas kernels for 0% -> 0%
where the time goes in v1:
time: 309 us; the launch traced here: 308 us
  waiting for transfers between devices  225 us (73%)
  local copies, waits for them, and re-layouts  31.9 us (10%)
  other arithmetic  21.7 us (7%)
  matrix products  15.2 us (5%)
  between operations  13.9 us (4%)
    all_gather x1, waiting for transfers between devices, body(): products = jnp.sum(lax.all_gather(partial_value, 'tm'), axis=0)  158 us
    all_gather x1, waiting for transfers between devices, body(): lax.all_gather(v_basis, 'vox', axis=1, tiled=True)  44 us
    reduce_scatter x1, waiting for transfers between devices, body(): lax.psum_scatter(partial_test, 'tm', scatter_dimension=0, tiled=True)  21.9 us
    all_gather x1, local copies, waits for them, and re-layouts, body(): products = jnp.sum(lax.all_gather(partial_value, 'tm'), axis=0)  20.7 us
    reduce_sum x1, other arithmetic, body(): products = jnp.sum(lax.all_gather(partial_value, 'tm'), axis=0)  15.1 us
    dot_general x1, matrix products, body(): lax.dot_general(u_train, responses, (((0,), (0,)), ((), ())), preferred_e...  6.6 us
    dot_general x1, matrix products, body(): jnp.dot(lax.all_gather(v_basis, 'vox', axis=1, tiled=True), filtered, pre...  6.38 us
  transfers between devices with their start and end apart: 3, of which 3 were waited for; matrix products, arithmetic and copies ran while one was open for 15% of the time, Pallas kernels for 0%

profile of v1, /device:TPU:0, one launch (start us, length us, event | category | flops | bytes accessed | tf_op | source)
XLA Modules:
  0.0 307.6 jit_solution(15315573392722801119)
XLA Ops:
  7.2 0.8 fusion.10
  8.0 0.7 sort.17
  8.8 1.3 copy.32
  10.1 0.3 copy.33
  10.4 1.3 gather_fusion
  11.8 1.2 copy.34
  12.9 0.1 broadcast_bitcast_fusion
  13.0 0.1 bitcast_select_fusion
  13.1 6.6 %convolution_bitcast_fusion = f32[4096,256]{0,1:T(8,128)} fusion(bf16[768,256]{0,1:T(8,128)(2,1)S(1)} %bitcast_select_fusion, bf16[768,4096]{1,0:T(8,128)(2,1)} %param.8), kind=kOutput, calls=%fused_computation.4 | convolution fusion | flops 1610612736 | bytes 10878976 | tf_op jit(solution)/shard_map/dot_general | solution.py:26
  19.8 0.0 all-gather.4.cloned.1.call-start
  19.8 0.7 all-gather.4.cloned.1.call-update
  20.6 0.1 fusion.5
  20.6 0.6 gather_fusion.1
  21.2 0.5 fusion.1
  21.7 158.2 %all-gather.6.cloned.1.call-done = f32[16384,256]{0,1:T(8,128)} async-done(((f32[4096,256]{0,1:T(8,128)}), f32[16384,256]{0,1:T(8,128)}) %all-gather.6.cloned.1.call-update) | async-done | bytes 16777232 | tf_op jit(solution)/shard_map/all_gather | solution.py:29
  179.9 20.7 %reshape.75 = f32[4,4096,256]{1,0,2:T(4,128)} reshape(f32[16384,256]{0,1:T(8,128)} %all-gather.6.cloned.1.call-done) | data formatting | bytes 33554432 | tf_op jit(solution)/shard_map/all_gather | solution.py:29
  200.7 15.1 %reduce_sum.9 = f32[4096,256]{0,1:T(8,128)} reduce(f32[4,4096,256]{1,0,2:T(4,128)} %reshape.75, f32[]{:T(128)} %constant.38.clone.1), dimensions={0}, to_apply=%region_1.2 | reduce | flops 3145728 | bytes 20971524 | tf_op jit(solution)/shard_map/reduce_sum | solution.py:29
  215.7 3.9 %fusion = bf16[4096,256]{0,1:T(8,128)(2,1)} fusion(f32[4096,256]{0,1:T(8,128)} %reduce_sum.9, f32[4096,2]{0,1:T(2,128)S(1)} %fusion.1), kind=kLoop, calls=%fused_computation.6 | loop fusion | flops 2097152 | bytes 6324224 | tf_op jit(solution)/shard_map/convert_element_type | solution.py:36
  219.6 44.0 %all-gather.4.cloned.1.call-done = bf16[1024,4096]{1,0:T(8,128)(2,1)} async-done(((bf16[1024,512]{1,0:T(8,128)(2,1)}), bf16[1024,4096]{1,0:T(8,128)(2,1)}) %all-gather.4.cloned.1.call-update) | async-done | bytes 8388624 | tf_op jit(solution)/shard_map/all_gather | solution.py:38
  263.6 6.4 %convolution_convert_fusion = bf16[256,1024]{1,0:T(8,128)(2,1)S(1)} fusion(bf16[4096,256]{0,1:T(8,128)(2,1)} %fusion, bf16[1024,4096]{1,0:T(8,128)(2,1)} %all-gather.4.cloned.1.call-done), kind=kOutput, calls=%fused_computation.8 | convolution fusion | flops 2147745792 | bytes 11010048 | tf_op jit(solution)/shard_map/dot_general | solution.py:37
  270.0 1.7 convolution_bitcast_fusion.1
  271.8 0.3 copy.35
  272.0 0.1 broadcast_in_dim.42
  272.1 0.7 scatter_fusion
  272.9 1.2 copy.36
  274.1 2.3 copy.39
  276.4 21.9 %reduce-scatter.2.cloned.1.call-done = f32[256,256]{0,1:T(8,128)} async-done(((f32[1024,256]{0,1:T(8,128)}), f32[256,256]{0,1:T(8,128)}) %reduce-scatter.2.cloned.1.call-update) | async-done | bytes 262160 | tf_op jit(solution)/shard_map/reduce_scatter | solution.py:44
  298.3 1.0 convert_element_type.21
  299.3 0.1 copy.37
  299.5 0.6 scatter_fusion.1
  300.1 0.1 copy.38
  300.2 0.8 copy.40
  (17 shorter events, 0.2 us)
Async XLA Ops:
  7.2 262.8 %copy-start = (bf16[1024,1024]{1,0:T(8,128)(2,1)S(1)}, bf16[1024,1024]{1,0:T(8,128)(2,1)}, u32[]{:S(2)}) copy-start(bf16[1024,1024]{1,0:T(8,128)(2,1)} %param.15) | copy-start | bytes 6291460
  7.2 172.7 %all-gather.6.cloned.1.call-start = ((), (), s32[]{:S(2)}) async-start(), calls=%async_computation.3 | async-start | bytes 20971520 | tf_op jit(solution)/shard_map/all_gather | solution.py:29
  19.7 0.8 copy-start.2
  19.7 1.5 copy-start.1
  19.7 1.5 copy-start.3
  19.8 243.8 %all-gather.4.cloned.1.call-start = ((), (), s32[]{:S(2)}) async-start(), calls=%async_computation.1 | async-start | bytes 9437184 | tf_op jit(solution)/shard_map/all_gather | solution.py:38
  20.5 277.8 %reduce-scatter.2.cloned.1.call-start = ((), (), s32[]{:S(2)}) async-start(), calls=%async_computation.2 | async-start | bytes 1310720 | tf_op jit(solution)/shard_map/reduce_scatter | solution.py:44
Sparse Core Ops, SparseCore 0:
  19.9 160.0 all-gather.5
  181.5 82.0 all-gather.3
  271.9 26.4 reduce-scatter.1
